TPU v7x, 512 devices: a whole 4x8x8 slice. The times are simulated.
512 devices in a mesh: exp: 16 (over y, core), space: 32 (over z, x).
Axes of the slice: x: 4, y: 8, z: 8, core: 2. Of those that a mesh axis runs over, the one named last changes fastest.
Arguments:
- initial: float32 [16, 4, 64, 64, 128], P('exp', None, 'space'), may hold values from -6 to 6
- cotangent: float32 [16, 4, 64, 64, 128], P('exp', None, 'space'), may hold values from -6 to 6
- permeability: float32 [64, 64, 128], P('space'), may hold values from 0.25 to 1.25
- labels: int32 [64, 64, 128], P('space'), may hold values from 0 to 511
- comp_scale: float32 [4], replicated, may hold values from 0.3 to 1
- coupling_mask: int32 [4, 4], replicated, may hold values from 0 to 1
- coupling_rate: float32 [4, 4], replicated, may hold values from 0.05 to 0.5
- dose: float32 [16], P('exp'), may hold values from 50 to 200
- inject_voxel: int32 [16], P('exp'), may hold values from 0 to 524287
- arrival: int32 [16], P('exp'), may hold values from 0 to 4
Outputs:
- concentration: float32 [16, 4, 64, 64, 128], P('exp', None, 'space')
- sensitivity: float32 [16, 4, 64, 64, 128], P('exp', None, 'space')
- perm_gradient: float32 [512], replicated
All inputs are finite; a program needn't handle non-finite values.
Results may differ from a plain program's by a relative error of at most 0.0003.
Values sent between devices are 32-bit elements; how exact they have to be, the bound alone decides.
No kernel may reach another device: no remote copies, remote signals or barrier semaphores. Data moves between devices by JAX's collectives and lax.ppermute only.
A program may use at most 64 MiB of HBM per device.

v0:
```python
import math
import jax
import jax.numpy as jnp
from jax import lax
from jax.sharding import PartitionSpec as P

STEPS = 5
LABELS = 512
time_step = 0.1


def extended(block, sides, width):
    for axis, dim in sides:
        count = lax.axis_size(axis)
        forward = [(i, i + 1) for i in range(count - 1)]
        backward = [(target, source) for source, target in forward]
        low = lax.ppermute(
            lax.slice_in_dim(block, block.shape[dim] - width, None, axis=dim), axis, forward
        )
        high = lax.ppermute(lax.slice_in_dim(block, 0, width, axis=dim), axis, backward)
        block = jnp.concatenate([low, block, high], axis=dim)
    return block


def sides(padded):
    return [
        padded[..., 2:, 1:-1, 1:-1],
        padded[..., :-2, 1:-1, 1:-1],
        padded[..., 1:-1, 2:, 1:-1],
        padded[..., 1:-1, :-2, 1:-1],
        padded[..., 1:-1, 1:-1, 2:],
        padded[..., 1:-1, 1:-1, :-2],
    ]


def widen(field):
    return jnp.pad(field, ((0, 0), (0, 0), (1, 1), (1, 1)))


def coupling(coupling_mask, coupling_rate):
    size = coupling_rate.shape[0]
    off = (
        coupling_mask.astype(jnp.float32) * coupling_rate * (1.0 - jnp.eye(size, dtype=jnp.float32))
    )
    return off - jnp.diag(jnp.sum(off, axis=1))


def on_device(
    initial,
    cotangent,
    permeability,
    labels,
    comp_scale,
    coupling_mask,
    coupling_rate,
    dose,
    inject_voxel,
    arrival,
):
    rows, wide, deep = permeability.shape
    perm_pad = extended(permeability, (("space", 0),), 1)
    perm_pad = jnp.pad(perm_pad, ((0, 0), (1, 1), (1, 1)))
    faces = [0.5 * (permeability + near) for near in sides(perm_pad)]
    mixing = coupling(coupling_mask, coupling_rate)
    scale = comp_scale[:, None, None, None]

    def laplace(padded, center):
        total = jnp.zeros_like(center)
        for coef, near in zip(faces, sides(padded)):
            total = total + coef * (near - center)
        return total

    offset = lax.axis_index("space") * rows
    plane_x = offset + lax.broadcasted_iota(jnp.int32, (rows, wide, deep), 0)
    plane_y = lax.broadcasted_iota(jnp.int32, (rows, wide, deep), 1)
    plane_z = lax.broadcasted_iota(jnp.int32, (rows, wide, deep), 2)
    flat = (plane_x * wide + plane_y) * deep + plane_z
    spot = (flat == inject_voxel[0]).astype(jnp.float32)
    state = initial[0]
    stored = []
    for step in range(STEPS):
        padded = widen(extended(state, (("space", 1),), 1))
        stored.append(padded)
        flow = scale * laplace(padded, state)
        flow = flow + jnp.einsum("cd,dxyz->cxyz", mixing, state, precision=lax.Precision.HIGHEST)
        pulse = jnp.where(step >= arrival[0], dose[0], 0.0) * time_step * spot
        state = state + time_step * flow
        state = state.at[0].add(pulse)
    adjoint = cotangent[0]
    grad = jnp.zeros((rows, wide, deep), jnp.float32)
    for step in reversed(range(STEPS)):
        padded_u = stored[step]
        padded_l = widen(extended(adjoint, (("space", 1),), 1))
        center_u = padded_u[:, 1:-1, 1:-1, 1:-1]
        product = jnp.zeros_like(adjoint)
        for near_l, near_u in zip(sides(padded_l), sides(padded_u)):
            product = product + (near_l - adjoint) * (near_u - center_u)
        grad = grad + jnp.sum(scale * product, axis=0)
        flow = scale * laplace(padded_l, adjoint)
        flow = flow + jnp.einsum("dc,dxyz->cxyz", mixing, adjoint, precision=lax.Precision.HIGHEST)
        adjoint = adjoint + time_step * flow
    weighted = -0.5 * time_step * grad * permeability
    flat_labels = labels.reshape(-1)
    summed = lax.psum(weighted, "exp")
    binned = jax.ops.segment_sum(summed.reshape(-1), flat_labels, num_segments=LABELS)
    total = lax.psum(binned, "space")
    norm_factor = math.sqrt(
        rows * lax.axis_size("space") * wide * deep * lax.axis_size("exp") / LABELS
    )
    return (state[None], adjoint[None], total / norm_factor)


def solution(mesh):
    return jax.shard_map(
        on_device,
        mesh=mesh,
        in_specs=(
            P("exp", None, "space", None, None),
            P("exp", None, "space", None, None),
            P("space", None, None),
            P("space", None, None),
            P(),
            P(),
            P(),
            P("exp"),
            P("exp"),
            P("exp"),
        ),
        out_specs=(P("exp", None, "space", None, None), P("exp", None, "space", None, None), P()),
        check_vma=False,
    )
```

profile of v0, /device:TPU:8, one launch (start us, length us, event | category | flops | bytes accessed | tf_op | source)
XLA Modules:
  0.0 471.1 jit_solution(2731218075138146100)
XLA Ops:
  7.2 0.8 fusion.79
  8.0 3.5 collective-permute-start.2
  11.6 1.4 collective-permute-start
  13.0 1.1 copy.36
  14.2 4.6 collective-permute-start.13
  18.8 1.3 collective-permute-start.12
  20.3 4.6 collective-permute-start.3
  27.0 1.3 collective-permute-start.1
  28.7 5.2 %collective-permute-done.1 = f32[4,1,64,128]{3,0,2,1:T(4,128)S(1)} collective-permute-done((f32[4,1,64,128]{3,0,2,1:T(4,128)S(1)}, f32[4,1,64,128]{3,0,2,1:T(4,128)S(1)}, u32[]{:S(2)}, u32[]{:S(2)}) %collective-permute-start.1) | collective-permute-done | bytes 131104 | tf_op jit(solution)/shard_map/ppermute | solution.py:20
  34.5 0.8 fusion.20
  35.5 1.3 scatter-add.24
  36.9 5.0 %collective-permute-start.5 = (f32[4,1,64,128]{3,0,2,1:T(4,128)S(1)}, f32[4,1,64,128]{3,0,2,1:T(4,128)S(1)}, u32[]{:S(2)}, u32[]{:S(2)}) collective-permute-start(f32[4,1,64,128]{3,0,2,1:T(4,128)S(1)} %get-tuple-element.86), channel_id=1, source_target_pairs={{0,1},{1,2},{2,3},{3,4},{4,5},{5,6},{6,7},{7,8},{8,9},{9,10},{10,1... | collective-permute-start | bytes 393224 | tf_op jit(solution)/shard_map/ppermute | solution.py:17
  41.9 1.3 collective-permute-start.4
  43.9 1.1 fusion.10
  45.1 0.7 fusion.72
  45.8 7.3 %collective-permute-start.15 = (f32[4,1,64,128]{3,0,2,1:T(4,128)}, f32[4,1,64,128]{3,0,2,1:T(4,128)}, u32[]{:S(2)}, u32[]{:S(2)}) collective-permute-start(f32[4,1,64,128]{3,0,2,1:T(4,128)} %get-tuple-element.76), channel_id=1, source_target_pairs={{0,1},{1,2},{2,3},{3,4},{4,5},{5,6},{6,7},{7,8},{8,9},{9,10},{10,1... | collective-permute-start | bytes 393224 | tf_op jit(solution)/shard_map/ppermute | solution.py:17
  53.1 1.3 collective-permute-start.14
  55.2 1.0 fusion.18
  56.9 0.8 slice_add_fusion.3
  57.7 2.8 scatter-add.25
  60.5 1.0 fusion.76
  61.5 6.0 %collective-permute-start.7 = (f32[4,1,64,128]{3,0,2,1:T(4,128)S(1)}, f32[4,1,64,128]{3,0,2,1:T(4,128)S(1)}, u32[]{:S(2)}, u32[]{:S(2)}) collective-permute-start(f32[4,1,64,128]{3,0,2,1:T(4,128)S(1)} %get-tuple-element.84), channel_id=1, source_target_pairs={{0,1},{1,2},{2,3},{3,4},{4,5},{5,6},{6,7},{7,8},{8,9},{9,10},{10,1... | collective-permute-start | bytes 393224 | tf_op jit(solution)/shard_map/ppermute | solution.py:17
  67.6 1.3 collective-permute-start.6
  68.9 1.7 select_maximum_fusion.6
  70.6 2.6 fusion.8
  73.2 0.8 fusion.71
  74.0 5.2 %collective-permute-start.17 = (f32[4,1,64,128]{3,0,2,1:T(4,128)}, f32[4,1,64,128]{3,0,2,1:T(4,128)}, u32[]{:S(2)}, u32[]{:S(2)}) collective-permute-start(f32[4,1,64,128]{3,0,2,1:T(4,128)} %get-tuple-element.74), channel_id=1, source_target_pairs={{0,1},{1,2},{2,3},{3,4},{4,5},{5,6},{6,7},{7,8},{8,9},{9,10},{10,1... | collective-permute-start | bytes 393224 | tf_op jit(solution)/shard_map/ppermute | solution.py:17
  79.2 1.5 collective-permute-start.16
  81.3 1.0 fusion.16
  82.4 0.7 copy-done.14
  83.1 0.8 slice_add_fusion.2
  83.9 2.8 scatter-add.26
  86.7 1.0 fusion.75
  87.7 4.6 collective-permute-start.9
  92.3 1.3 collective-permute-start.8
  93.6 1.7 select_maximum_fusion.4
  95.4 2.3 fusion.6
  97.7 0.8 fusion.70
  98.4 6.8 %collective-permute-start.19 = (f32[4,1,64,128]{3,0,2,1:T(4,128)}, f32[4,1,64,128]{3,0,2,1:T(4,128)}, u32[]{:S(2)}, u32[]{:S(2)}) collective-permute-start(f32[4,1,64,128]{3,0,2,1:T(4,128)} %get-tuple-element.72), channel_id=1, source_target_pairs={{0,1},{1,2},{2,3},{3,4},{4,5},{5,6},{6,7},{7,8},{8,9},{9,10},{10,1... | collective-permute-start | bytes 393224 | tf_op jit(solution)/shard_map/ppermute | solution.py:17
  105.2 1.4 collective-permute-start.18
  106.7 2.5 multiply_reduce_fusion.2
  109.8 1.0 fusion.14
  111.5 0.8 slice_add_fusion.1
  112.3 2.8 scatter-add.29
  115.2 1.0 fusion.74
  116.2 6.0 %collective-permute-start.11 = (f32[4,1,64,128]{3,0,2,1:T(4,128)S(1)}, f32[4,1,64,128]{3,0,2,1:T(4,128)S(1)}, u32[]{:S(2)}, u32[]{:S(2)}) collective-permute-start(f32[4,1,64,128]{3,0,2,1:T(4,128)S(1)} %get-tuple-element.80), channel_id=1, source_target_pairs={{0,1},{1,2},{2,3},{3,4},{4,5},{5,6},{6,7},{7,8},{8,9},{9,10},{10,1... | collective-permute-start | bytes 393224 | tf_op jit(solution)/shard_map/ppermute | solution.py:17
  122.3 1.3 collective-permute-start.10
  123.6 1.7 select_maximum_fusion.2
  125.4 2.3 fusion.4
  127.7 6.7 %collective-permute-start.21 = (f32[4,1,64,128]{3,0,2,1:T(4,128)S(1)}, f32[4,1,64,128]{3,0,2,1:T(4,128)S(1)}, u32[]{:S(2)}, u32[]{:S(2)}) collective-permute-start(f32[4,1,64,128]{3,0,2,1:T(4,128)S(1)} %get-tuple-element.70), channel_id=1, source_target_pairs={{0,1},{1,2},{2,3},{3,4},{4,5},{5,6},{6,7},{7,8},{8,9},{9,10},{10,1... | collective-permute-start | bytes 393224 | tf_op jit(solution)/shard_map/ppermute | solution.py:17
  134.4 1.6 collective-permute-start.20
  136.1 1.9 multiply_reduce_fusion.3
  138.0 1.9 multiply_reduce_fusion.1
  141.1 0.9 multiply_reduce_fusion.4
  142.1 1.4 collective-permute-done.20
  144.2 0.9 multiply_reduce_fusion
  145.9 2.2 fusion.12
  148.2 1.1 fusion.2
  149.5 1.3 scatter-add.36
  150.8 0.7 copy.21
  151.6 0.7 copy.22
  152.3 122.5 %all-reduce.13.cloned.1.call-done = f32[16384]{0:T(1024)} async-done(((f32[16384]{0:T(1024)}), f32[16384]{0:T(1024)}) %all-reduce.13.cloned.1.call-update) | async-done | bytes 65552 | tf_op jit(solution)/shard_map/psum | solution.py:104
  274.8 113.6 %scatter_custom_fusion = f32[512]{0:T(512)S(1)} fusion(s32[16384]{0:T(1024)} %bitcast.74, f32[16384]{0:T(1024)} %all-reduce.13.cloned.1.call-done, f32[]{:T(128)} %constant.150.clone.1), kind=kCustom, calls=%fused_computation.191 | custom fusion | flops 16384 | bytes 2560 | tf_op jit(solution)/shard_map/scatter-add | solution.py:105
  388.3 75.4 %psum.15 = f32[512]{0:T(512)S(1)} all-reduce(f32[512]{0:T(512)S(1)} %scatter_custom_fusion), channel_id=1, replica_groups=mesh['exp'=16,'space'=32] {'space'}, use_global_device_ids=true, to_apply=%region_8.9 | all-reduce | flops 512 | bytes 4096 | tf_op jit(solution)/shard_map/psum | solution.py:106
  (236 shorter events, 8.9 us)
Async XLA Ops:
  7.2 12.9 %copy-start.57 = (f32[1,4,2,64,128]{4,3,2,1,0:T(8,128)S(1)}, f32[1,4,2,64,128]{4,3,2,1,0:T(8,128)}, u32[]{:S(2)}) copy-start(f32[1,4,2,64,128]{4,3,2,1,0:T(8,128)} %param.20) | copy-start | bytes 786436
  7.2 267.6 %all-reduce.13.cloned.1.call-start = ((), (), s32[]{:S(2)}) async-start(), calls=%async_computation | async-start | bytes 131072 | tf_op jit(solution)/shard_map/psum | solution.py:104
  8.0 16.8 %copy-start.95 = (f32[4,4]{1,0:T(4,128)S(1)}, f32[4,4]{1,0:T(4,128)}, u32[]{:S(2)}) copy-start(f32[4,4]{1,0:T(4,128)} %param.26) | copy-start | bytes 196
  8.0 16.8 %copy-start.96 = (s32[4,4]{1,0:T(4,128)S(1)}, s32[4,4]{1,0:T(4,128)}, u32[]{:S(2)}) copy-start(s32[4,4]{1,0:T(4,128)} %param.25) | copy-start | bytes 196
  8.0 19.0 %collective-permute-start.2 = (f32[1,64,128]{2,1,0:T(8,128)S(1)}, f32[1,64,128]{2,1,0:T(8,128)S(1)}, u32[]{:S(2)}, u32[]{:S(2)}) collective-permute-start(f32[1,64,128]{2,1,0:T(8,128)S(1)} %get-tuple-element.92), channel_id=1, source_target_pairs={{0,1},{1,2},{2,3},{3,4},{4,5},{5,6},{6,7},{7,8},{8,9},{9,10},{10,1... | collective-permute-start | bytes 98312 | tf_op jit(solution)/shard_map/ppermute | solution.py:17
  11.6 16.8 %copy-start.28 = (f32[2,64,128]{2,1,0:T(8,128)S(1)}, f32[2,64,128]{2,1,0:T(8,128)}, u32[]{:S(2)}) copy-start(f32[2,64,128]{2,1,0:T(8,128)} %param.22) | copy-start | bytes 196612
  11.6 16.7 %collective-permute-start = (f32[1,64,128]{2,1,0:T(8,128)S(1)}, f32[1,64,128]{2,1,0:T(8,128)S(1)}, u32[]{:S(2)}, u32[]{:S(2)}) collective-permute-start(f32[1,64,128]{2,1,0:T(8,128)S(1)} %get-tuple-element.93), channel_id=1, source_target_pairs={{1,0},{2,1},{3,2},{4,3},{5,4},{6,5},{7,6},{8,7},{9,8},{10,9},{11,1... | collective-permute-start | bytes 98312 | tf_op jit(solution)/shard_map/ppermute | solution.py:20
  14.2 29.7 %copy-start.6 = (f32[1,4,2,64,128]{4,1,3,2,0:T(4,128)}, f32[1,4,2,64,128]{4,1,3,2,0:T(4,128)S(1)}, u32[]{:S(2)}) copy-start(f32[1,4,2,64,128]{4,1,3,2,0:T(4,128)S(1)} %copy.36) | copy-start | bytes 786436
  14.2 29.0 %collective-permute-start.13 = (f32[4,1,64,128]{3,0,2,1:T(4,128)S(1)}, f32[4,1,64,128]{3,0,2,1:T(4,128)S(1)}, u32[]{:S(2)}, u32[]{:S(2)}) collective-permute-start(f32[4,1,64,128]{3,0,2,1:T(4,128)S(1)} %get-tuple-element.78), channel_id=1, source_target_pairs={{0,1},{1,2},{2,3},{3,4},{4,5},{5,6},{6,7},{7,8},{8,9},{9,10},{10,1... | collective-permute-start | bytes 393224 | tf_op jit(solution)/shard_map/ppermute | solution.py:17
  18.8 24.5 %collective-permute-start.12 = (f32[4,1,64,128]{3,0,2,1:T(4,128)S(1)}, f32[4,1,64,128]{3,0,2,1:T(4,128)S(1)}, u32[]{:S(2)}, u32[]{:S(2)}) collective-permute-start(f32[4,1,64,128]{3,0,2,1:T(4,128)S(1)} %get-tuple-element.79), channel_id=1, source_target_pairs={{1,0},{2,1},{3,2},{4,3},{5,4},{6,5},{7,6},{8,7},{9,8},{10,9},{11,1... | collective-permute-start | bytes 393224 | tf_op jit(solution)/shard_map/ppermute | solution.py:20
  20.3 8.4 %collective-permute-start.3 = (f32[4,1,64,128]{3,0,2,1:T(4,128)S(1)}, f32[4,1,64,128]{3,0,2,1:T(4,128)S(1)}, u32[]{:S(2)}, u32[]{:S(2)}) collective-permute-start(f32[4,1,64,128]{3,0,2,1:T(4,128)S(1)} %get-tuple-element.88), channel_id=1, source_target_pairs={{0,1},{1,2},{2,3},{3,4},{4,5},{5,6},{6,7},{7,8},{8,9},{9,10},{10,1... | collective-permute-start | bytes 393224 | tf_op jit(solution)/shard_map/ppermute | solution.py:17
  27.0 6.9 %collective-permute-start.1 = (f32[4,1,64,128]{3,0,2,1:T(4,128)S(1)}, f32[4,1,64,128]{3,0,2,1:T(4,128)S(1)}, u32[]{:S(2)}, u32[]{:S(2)}) collective-permute-start(f32[4,1,64,128]{3,0,2,1:T(4,128)S(1)} %get-tuple-element.89), channel_id=1, source_target_pairs={{1,0},{2,1},{3,2},{4,3},{5,4},{6,5},{7,6},{8,7},{9,8},{10,9},{11,1... | collective-permute-start | bytes 393224 | tf_op jit(solution)/shard_map/ppermute | solution.py:20
  28.6 15.2 %copy-start.58 = (f32[2,64,128]{2,1,0:T(8,128)}, f32[2,64,128]{2,1,0:T(8,128)S(1)}, u32[]{:S(2)}) copy-start(f32[2,64,128]{2,1,0:T(8,128)S(1)} %get-tuple-element.66) | copy-start | bytes 196612
  28.7 15.2 %copy-start.64 = (f32[2,64,128]{2,1,0:T(8,128)}, f32[2,64,128]{2,1,0:T(8,128)S(1)}, u32[]{:S(2)}) copy-start(f32[2,64,128]{2,1,0:T(8,128)S(1)} %get-tuple-element.67) | copy-start | bytes 196612
  28.7 15.2 %copy-start.70 = (f32[2,64,128]{2,1,0:T(8,128)}, f32[2,64,128]{2,1,0:T(8,128)S(1)}, u32[]{:S(2)}) copy-start(f32[2,64,128]{2,1,0:T(8,128)S(1)} %get-tuple-element.68) | copy-start | bytes 196612
  28.7 15.2 %copy-start.76 = (f32[2,64,128]{2,1,0:T(8,128)}, f32[2,64,128]{2,1,0:T(8,128)S(1)}, u32[]{:S(2)}) copy-start(f32[2,64,128]{2,1,0:T(8,128)S(1)} %get-tuple-element.69) | copy-start | bytes 196612
  28.7 15.2 %copy-start.82 = (f32[2,64,128]{2,1,0:T(8,128)}, f32[2,64,128]{2,1,0:T(8,128)S(1)}, u32[]{:S(2)}) copy-start(f32[2,64,128]{2,1,0:T(8,128)S(1)} %get-tuple-element.90) | copy-start | bytes 196612
  28.7 15.2 %copy-start.88 = (f32[2,64,128]{2,1,0:T(8,128)}, f32[2,64,128]{2,1,0:T(8,128)S(1)}, u32[]{:S(2)}) copy-start(f32[2,64,128]{2,1,0:T(8,128)S(1)} %get-tuple-element.91) | copy-start | bytes 196612
  36.9 17.5 %collective-permute-start.5 = (f32[4,1,64,128]{3,0,2,1:T(4,128)S(1)}, f32[4,1,64,128]{3,0,2,1:T(4,128)S(1)}, u32[]{:S(2)}, u32[]{:S(2)}) collective-permute-start(f32[4,1,64,128]{3,0,2,1:T(4,128)S(1)} %get-tuple-element.86), channel_id=1, source_target_pairs={{0,1},{1,2},{2,3},{3,4},{4,5},{5,6},{6,7},{7,8},{8,9},{9,10},{10,1... | collective-permute-start | bytes 393224 | tf_op jit(solution)/shard_map/ppermute | solution.py:17
  41.9 12.6 %collective-permute-start.4 = (f32[4,1,64,128]{3,0,2,1:T(4,128)S(1)}, f32[4,1,64,128]{3,0,2,1:T(4,128)S(1)}, u32[]{:S(2)}, u32[]{:S(2)}) collective-permute-start(f32[4,1,64,128]{3,0,2,1:T(4,128)S(1)} %get-tuple-element.87), channel_id=1, source_target_pairs={{1,0},{2,1},{3,2},{4,3},{5,4},{6,5},{7,6},{8,7},{9,8},{10,9},{11,1... | collective-permute-start | bytes 393224 | tf_op jit(solution)/shard_map/ppermute | solution.py:20
  43.9 10.6 %copy-start.9 = (f32[4,2,64,128]{3,0,2,1:T(4,128)S(1)}, f32[4,2,64,128]{3,0,2,1:T(4,128)}, u32[]{:S(2)}) copy-start(f32[4,2,64,128]{3,0,2,1:T(4,128)} %copy-done.8) | copy-start | bytes 786436
  45.1 10.0 %copy-start.59 = (f32[2,64,128]{2,1,0:T(8,128)S(1)}, f32[2,64,128]{2,1,0:T(8,128)}, u32[]{:S(2)}) copy-start(f32[2,64,128]{2,1,0:T(8,128)} %copy-done.58) | copy-start | bytes 196612
  45.1 10.0 %copy-start.65 = (f32[2,64,128]{2,1,0:T(8,128)S(1)}, f32[2,64,128]{2,1,0:T(8,128)}, u32[]{:S(2)}) copy-start(f32[2,64,128]{2,1,0:T(8,128)} %copy-done.64) | copy-start | bytes 196612
  45.1 10.0 %copy-start.71 = (f32[2,64,128]{2,1,0:T(8,128)S(1)}, f32[2,64,128]{2,1,0:T(8,128)}, u32[]{:S(2)}) copy-start(f32[2,64,128]{2,1,0:T(8,128)} %copy-done.70) | copy-start | bytes 196612
  45.8 23.0 %collective-permute-start.15 = (f32[4,1,64,128]{3,0,2,1:T(4,128)}, f32[4,1,64,128]{3,0,2,1:T(4,128)}, u32[]{:S(2)}, u32[]{:S(2)}) collective-permute-start(f32[4,1,64,128]{3,0,2,1:T(4,128)} %get-tuple-element.76), channel_id=1, source_target_pairs={{0,1},{1,2},{2,3},{3,4},{4,5},{5,6},{6,7},{7,8},{8,9},{9,10},{10,1... | collective-permute-start | bytes 393224 | tf_op jit(solution)/shard_map/ppermute | solution.py:17
  53.1 15.7 %collective-permute-start.14 = (f32[4,1,64,128]{3,0,2,1:T(4,128)}, f32[4,1,64,128]{3,0,2,1:T(4,128)}, u32[]{:S(2)}, u32[]{:S(2)}) collective-permute-start(f32[4,1,64,128]{3,0,2,1:T(4,128)} %get-tuple-element.77), channel_id=1, source_target_pairs={{1,0},{2,1},{3,2},{4,3},{5,4},{6,5},{7,6},{8,7},{9,8},{10,9},{11,1... | collective-permute-start | bytes 393224 | tf_op jit(solution)/shard_map/ppermute | solution.py:20
  60.4 10.1 %copy-start.20 = (f32[4,2,64,128]{3,0,2,1:T(4,128)S(1)}, f32[4,2,64,128]{3,0,2,1:T(4,128)}, u32[]{:S(2)}) copy-start(f32[4,2,64,128]{3,0,2,1:T(4,128)} %copy-done.19) | copy-start | bytes 786436
  60.4 10.1 %copy-start.60 = (f32[2,64,128]{2,1,0:T(8,128)S(1)}, f32[2,64,128]{2,1,0:T(8,128)}, u32[]{:S(2)}) copy-start(f32[2,64,128]{2,1,0:T(8,128)} %copy-done.58) | copy-start | bytes 196612
  60.4 10.1 %copy-start.66 = (f32[2,64,128]{2,1,0:T(8,128)S(1)}, f32[2,64,128]{2,1,0:T(8,128)}, u32[]{:S(2)}) copy-start(f32[2,64,128]{2,1,0:T(8,128)} %copy-done.64) | copy-start | bytes 196612
  60.4 10.1 %copy-start.72 = (f32[2,64,128]{2,1,0:T(8,128)S(1)}, f32[2,64,128]{2,1,0:T(8,128)}, u32[]{:S(2)}) copy-start(f32[2,64,128]{2,1,0:T(8,128)} %copy-done.70) | copy-start | bytes 196612
  60.5 10.1 %copy-start.78 = (f32[2,64,128]{2,1,0:T(8,128)S(1)}, f32[2,64,128]{2,1,0:T(8,128)}, u32[]{:S(2)}) copy-start(f32[2,64,128]{2,1,0:T(8,128)} %copy-done.76) | copy-start | bytes 196612
  60.5 10.1 %copy-start.84 = (f32[2,64,128]{2,1,0:T(8,128)S(1)}, f32[2,64,128]{2,1,0:T(8,128)}, u32[]{:S(2)}) copy-start(f32[2,64,128]{2,1,0:T(8,128)} %copy-done.82) | copy-start | bytes 196612
  60.5 10.1 %copy-start.90 = (f32[2,64,128]{2,1,0:T(8,128)S(1)}, f32[2,64,128]{2,1,0:T(8,128)}, u32[]{:S(2)}) copy-start(f32[2,64,128]{2,1,0:T(8,128)} %copy-done.88) | copy-start | bytes 196612
  61.5 19.1 %collective-permute-start.7 = (f32[4,1,64,128]{3,0,2,1:T(4,128)S(1)}, f32[4,1,64,128]{3,0,2,1:T(4,128)S(1)}, u32[]{:S(2)}, u32[]{:S(2)}) collective-permute-start(f32[4,1,64,128]{3,0,2,1:T(4,128)S(1)} %get-tuple-element.84), channel_id=1, source_target_pairs={{0,1},{1,2},{2,3},{3,4},{4,5},{5,6},{6,7},{7,8},{8,9},{9,10},{10,1... | collective-permute-start | bytes 393224 | tf_op jit(solution)/shard_map/ppermute | solution.py:17
  67.6 13.1 %collective-permute-start.6 = (f32[4,1,64,128]{3,0,2,1:T(4,128)S(1)}, f32[4,1,64,128]{3,0,2,1:T(4,128)S(1)}, u32[]{:S(2)}, u32[]{:S(2)}) collective-permute-start(f32[4,1,64,128]{3,0,2,1:T(4,128)S(1)} %get-tuple-element.85), channel_id=1, source_target_pairs={{1,0},{2,1},{3,2},{4,3},{5,4},{6,5},{7,6},{8,7},{9,8},{10,9},{11,1... | collective-permute-start | bytes 393224 | tf_op jit(solution)/shard_map/ppermute | solution.py:20
  70.6 10.1 %copy-start.12 = (f32[4,2,64,128]{3,0,2,1:T(4,128)S(1)}, f32[4,2,64,128]{3,0,2,1:T(4,128)}, u32[]{:S(2)}) copy-start(f32[4,2,64,128]{3,0,2,1:T(4,128)} %scatter-add.25) | copy-start | bytes 786436
  74.0 19.6 %collective-permute-start.17 = (f32[4,1,64,128]{3,0,2,1:T(4,128)}, f32[4,1,64,128]{3,0,2,1:T(4,128)}, u32[]{:S(2)}, u32[]{:S(2)}) collective-permute-start(f32[4,1,64,128]{3,0,2,1:T(4,128)} %get-tuple-element.74), channel_id=1, source_target_pairs={{0,1},{1,2},{2,3},{3,4},{4,5},{5,6},{6,7},{7,8},{8,9},{9,10},{10,1... | collective-permute-start | bytes 393224 | tf_op jit(solution)/shard_map/ppermute | solution.py:17
  79.2 14.4 %collective-permute-start.16 = (f32[4,1,64,128]{3,0,2,1:T(4,128)}, f32[4,1,64,128]{3,0,2,1:T(4,128)}, u32[]{:S(2)}, u32[]{:S(2)}) collective-permute-start(f32[4,1,64,128]{3,0,2,1:T(4,128)} %get-tuple-element.75), channel_id=1, source_target_pairs={{1,0},{2,1},{3,2},{4,3},{5,4},{6,5},{7,6},{8,7},{9,8},{10,9},{11,1... | collective-permute-start | bytes 393224 | tf_op jit(solution)/shard_map/ppermute | solution.py:20
  87.7 21.4 %collective-permute-start.9 = (f32[4,1,64,128]{3,0,2,1:T(4,128)S(1)}, f32[4,1,64,128]{3,0,2,1:T(4,128)S(1)}, u32[]{:S(2)}, u32[]{:S(2)}) collective-permute-start(f32[4,1,64,128]{3,0,2,1:T(4,128)S(1)} %get-tuple-element.82), channel_id=1, source_target_pairs={{0,1},{1,2},{2,3},{3,4},{4,5},{5,6},{6,7},{7,8},{8,9},{9,10},{10,1... | collective-permute-start | bytes 393224 | tf_op jit(solution)/shard_map/ppermute | solution.py:17
  92.3 16.9 %collective-permute-start.8 = (f32[4,1,64,128]{3,0,2,1:T(4,128)S(1)}, f32[4,1,64,128]{3,0,2,1:T(4,128)S(1)}, u32[]{:S(2)}, u32[]{:S(2)}) collective-permute-start(f32[4,1,64,128]{3,0,2,1:T(4,128)S(1)} %get-tuple-element.83), channel_id=1, source_target_pairs={{1,0},{2,1},{3,2},{4,3},{5,4},{6,5},{7,6},{8,7},{9,8},{10,9},{11,1... | collective-permute-start | bytes 393224 | tf_op jit(solution)/shard_map/ppermute | solution.py:20
  95.4 11.3 %copy-start.5 = (f32[4,4,66,130]{3,0,2,1:T(4,128)S(1)}, f32[4,4,66,130]{3,0,2,1:T(4,128)}, u32[]{:S(2)}) copy-start(f32[4,4,66,130]{3,0,2,1:T(4,128)} %copy-done.4) | copy-start | bytes 1647364
  95.4 11.3 %copy-start.13 = (f32[4,2,64,128]{3,0,2,1:T(4,128)S(1)}, f32[4,2,64,128]{3,0,2,1:T(4,128)}, u32[]{:S(2)}) copy-start(f32[4,2,64,128]{3,0,2,1:T(4,128)} %scatter-add.25) | copy-start | bytes 786436
  95.4 11.3 %copy-start.51 = (f32[4,1,64,128]{3,0,2,1:T(4,128)S(1)}, f32[4,1,64,128]{3,0,2,1:T(4,128)}, u32[]{:S(2)}) copy-start(f32[4,1,64,128]{3,0,2,1:T(4,128)} %copy-done.50) | copy-start | bytes 393220
  95.4 11.3 %copy-start.55 = (f32[4,1,64,128]{3,0,2,1:T(4,128)S(1)}, f32[4,1,64,128]{3,0,2,1:T(4,128)}, u32[]{:S(2)}) copy-start(f32[4,1,64,128]{3,0,2,1:T(4,128)} %copy-done.54) | copy-start | bytes 393220
  98.4 25.1 %collective-permute-start.19 = (f32[4,1,64,128]{3,0,2,1:T(4,128)}, f32[4,1,64,128]{3,0,2,1:T(4,128)}, u32[]{:S(2)}, u32[]{:S(2)}) collective-permute-start(f32[4,1,64,128]{3,0,2,1:T(4,128)} %get-tuple-element.72), channel_id=1, source_target_pairs={{0,1},{1,2},{2,3},{3,4},{4,5},{5,6},{6,7},{7,8},{8,9},{9,10},{10,1... | collective-permute-start | bytes 393224 | tf_op jit(solution)/shard_map/ppermute | solution.py:17
  105.2 18.4 %collective-permute-start.18 = (f32[4,1,64,128]{3,0,2,1:T(4,128)}, f32[4,1,64,128]{3,0,2,1:T(4,128)}, u32[]{:S(2)}, u32[]{:S(2)}) collective-permute-start(f32[4,1,64,128]{3,0,2,1:T(4,128)} %get-tuple-element.73), channel_id=1, source_target_pairs={{1,0},{2,1},{3,2},{4,3},{5,4},{6,5},{7,6},{8,7},{9,8},{10,9},{11,1... | collective-permute-start | bytes 393224 | tf_op jit(solution)/shard_map/ppermute | solution.py:20
  115.1 10.1 %copy-start.25 = (f32[4,2,64,128]{3,0,2,1:T(4,128)S(1)}, f32[4,2,64,128]{3,0,2,1:T(4,128)}, u32[]{:S(2)}) copy-start(f32[4,2,64,128]{3,0,2,1:T(4,128)} %copy-done.24) | copy-start | bytes 786436
  115.1 10.1 %copy-start.62 = (f32[2,64,128]{2,1,0:T(8,128)S(1)}, f32[2,64,128]{2,1,0:T(8,128)}, u32[]{:S(2)}) copy-start(f32[2,64,128]{2,1,0:T(8,128)} %copy-done.58) | copy-start | bytes 196612
  115.1 10.2 %copy-start.68 = (f32[2,64,128]{2,1,0:T(8,128)S(1)}, f32[2,64,128]{2,1,0:T(8,128)}, u32[]{:S(2)}) copy-start(f32[2,64,128]{2,1,0:T(8,128)} %copy-done.64) | copy-start | bytes 196612
  115.1 10.2 %copy-start.74 = (f32[2,64,128]{2,1,0:T(8,128)S(1)}, f32[2,64,128]{2,1,0:T(8,128)}, u32[]{:S(2)}) copy-start(f32[2,64,128]{2,1,0:T(8,128)} %copy-done.70) | copy-start | bytes 196612
  115.1 10.2 %copy-start.80 = (f32[2,64,128]{2,1,0:T(8,128)S(1)}, f32[2,64,128]{2,1,0:T(8,128)}, u32[]{:S(2)}) copy-start(f32[2,64,128]{2,1,0:T(8,128)} %copy-done.76) | copy-start | bytes 196612
  115.1 10.2 %copy-start.86 = (f32[2,64,128]{2,1,0:T(8,128)S(1)}, f32[2,64,128]{2,1,0:T(8,128)}, u32[]{:S(2)}) copy-start(f32[2,64,128]{2,1,0:T(8,128)} %copy-done.82) | copy-start | bytes 196612
  115.2 10.2 %copy-start.92 = (f32[2,64,128]{2,1,0:T(8,128)S(1)}, f32[2,64,128]{2,1,0:T(8,128)}, u32[]{:S(2)}) copy-start(f32[2,64,128]{2,1,0:T(8,128)} %copy-done.88) | copy-start | bytes 196612
  116.2 23.8 %collective-permute-start.11 = (f32[4,1,64,128]{3,0,2,1:T(4,128)S(1)}, f32[4,1,64,128]{3,0,2,1:T(4,128)S(1)}, u32[]{:S(2)}, u32[]{:S(2)}) collective-permute-start(f32[4,1,64,128]{3,0,2,1:T(4,128)S(1)} %get-tuple-element.80), channel_id=1, source_target_pairs={{0,1},{1,2},{2,3},{3,4},{4,5},{5,6},{6,7},{7,8},{8,9},{9,10},{10,1... | collective-permute-start | bytes 393224 | tf_op jit(solution)/shard_map/ppermute | solution.py:17
  122.3 17.7 %collective-permute-start.10 = (f32[4,1,64,128]{3,0,2,1:T(4,128)S(1)}, f32[4,1,64,128]{3,0,2,1:T(4,128)S(1)}, u32[]{:S(2)}, u32[]{:S(2)}) collective-permute-start(f32[4,1,64,128]{3,0,2,1:T(4,128)S(1)} %get-tuple-element.81), channel_id=1, source_target_pairs={{1,0},{2,1},{3,2},{4,3},{5,4},{6,5},{7,6},{8,7},{9,8},{10,9},{11,1... | collective-permute-start | bytes 393224 | tf_op jit(solution)/shard_map/ppermute | solution.py:20
  125.3 10.8 %copy-start.1 = (f32[4,4,66,130]{3,0,2,1:T(4,128)S(1)}, f32[4,4,66,130]{3,0,2,1:T(4,128)}, u32[]{:S(2)}) copy-start(f32[4,4,66,130]{3,0,2,1:T(4,128)} %copy-done) | copy-start | bytes 1647364
  125.3 10.8 %copy-start.3 = (f32[4,4,66,130]{3,0,2,1:T(4,128)S(1)}, f32[4,4,66,130]{3,0,2,1:T(4,128)}, u32[]{:S(2)}) copy-start(f32[4,4,66,130]{3,0,2,1:T(4,128)} %copy-done.2) | copy-start | bytes 1647364
  125.3 10.8 %copy-start.16 = (f32[4,2,64,128]{3,0,2,1:T(4,128)S(1)}, f32[4,2,64,128]{3,0,2,1:T(4,128)}, u32[]{:S(2)}) copy-start(f32[4,2,64,128]{3,0,2,1:T(4,128)} %scatter-add.26) | copy-start | bytes 786436
  125.3 10.8 %copy-start.21 = (f32[4,2,64,128]{3,0,2,1:T(4,128)S(1)}, f32[4,2,64,128]{3,0,2,1:T(4,128)}, u32[]{:S(2)}) copy-start(f32[4,2,64,128]{3,0,2,1:T(4,128)} %copy-done.19) | copy-start | bytes 786436
  125.4 10.8 %copy-start.43 = (f32[4,1,64,128]{3,0,2,1:T(4,128)S(1)}, f32[4,1,64,128]{3,0,2,1:T(4,128)}, u32[]{:S(2)}) copy-start(f32[4,1,64,128]{3,0,2,1:T(4,128)} %copy-done.42) | copy-start | bytes 393220
  125.4 10.8 %copy-start.46 = (f32[4,1,64,128]{3,0,2,1:T(4,128)S(1)}, f32[4,1,64,128]{3,0,2,1:T(4,128)}, u32[]{:S(2)}) copy-start(f32[4,1,64,128]{3,0,2,1:T(4,128)} %copy-done.45) | copy-start | bytes 393220
  127.7 16.5 %copy-start.22 = (f32[4,2,64,128]{3,0,2,1:T(4,128)}, f32[4,2,64,128]{3,0,2,1:T(4,128)S(1)}, u32[]{:S(2)}) copy-start(f32[4,2,64,128]{3,0,2,1:T(4,128)S(1)} %fusion.4) | copy-start | bytes 786436
  127.7 14.3 %collective-permute-start.21 = (f32[4,1,64,128]{3,0,2,1:T(4,128)S(1)}, f32[4,1,64,128]{3,0,2,1:T(4,128)S(1)}, u32[]{:S(2)}, u32[]{:S(2)}) collective-permute-start(f32[4,1,64,128]{3,0,2,1:T(4,128)S(1)} %get-tuple-element.70), channel_id=1, source_target_pairs={{0,1},{1,2},{2,3},{3,4},{4,5},{5,6},{6,7},{7,8},{8,9},{9,10},{10,1... | collective-permute-start | bytes 393224 | tf_op jit(solution)/shard_map/ppermute | solution.py:17
  134.4 9.1 %collective-permute-start.20 = (f32[4,1,64,128]{3,0,2,1:T(4,128)S(1)}, f32[4,1,64,128]{3,0,2,1:T(4,128)S(1)}, u32[]{:S(2)}, u32[]{:S(2)}) collective-permute-start(f32[4,1,64,128]{3,0,2,1:T(4,128)S(1)} %get-tuple-element.71), channel_id=1, source_target_pairs={{1,0},{2,1},{3,2},{4,3},{5,4},{6,5},{7,6},{8,7},{9,8},{10,9},{11,1... | collective-permute-start | bytes 393224 | tf_op jit(solution)/shard_map/ppermute | solution.py:20
  (56 other events, 212.9 us)
Sparse Core Ops, SparseCore 0:
  145.9 128.7 all-reduce.12
where the time goes:
time: 472 us; the launch traced here: 471 us
  other arithmetic  135 us (29%)
  waiting for transfers between devices  129 us (27%)
  blocking collectives  75.4 us (16%)
  starting transfers between devices  75.2 us (16%)
  local copies, waits for them, and re-layouts  23 us (5%)
  between operations  17.9 us (4%)
  matrix products  15.3 us (3%)
    psum x1, waiting for transfers between devices, on_device(): summed = lax.psum(weighted, 'exp')  122 us
    scatter-add x1, other arithmetic, on_device(): jax.ops.segment_sum(summed.reshape(-1), flat_labels, num_segments=LABELS)  114 us
    psum x1, blocking collectives, on_device(): total = lax.psum(binned, 'space')  75.4 us
    ppermute x11, starting transfers between devices, extended(): lax.ppermute(lax.slice_in_dim(block, block.shape[dim] - width, None, axis...  60.2 us
    ppermute x11, starting transfers between devices, extended(): lax.ppermute(lax.slice_in_dim(block, 0, width, axis=dim), axis, backward)  15 us
    scatter-add x5, local copies, waits for them, and re-layouts, on_device(): state = state.at[0].add(pulse)  11 us
  transfers between devices with their start and end apart: 23, of which 3 were waited for; matrix products, arithmetic and copies ran while one was open for 11% of the time, Pallas kernels for 0%

commit v1 on v0

--- a/solution.py
+++ b/solution.py
@@ -101,7 +101,8 @@
         adjoint = adjoint + time_step * flow
     weighted = -0.5 * time_step * grad * permeability
     flat_labels = labels.reshape(-1)
-    summed = lax.psum(weighted, "exp")
+    shards = lax.all_gather(weighted, "exp", axis=0, tiled=False)
+    summed = shards.sum(axis=0)
     binned = jax.ops.segment_sum(summed.reshape(-1), flat_labels, num_segments=LABELS)
     total = lax.psum(binned, "space")
     norm_factor = math.sqrt(

time: 472 us -> 411 us (0.87)
  the two profiles are of different devices: /device:TPU:8 before, /device:TPU:24 now
where the time goes in v1:
time: 411 us; the launch traced here: 409 us
  other arithmetic  137 us (33%)
  blocking collectives  75.7 us (18%)
  starting transfers between devices  75 us (18%)
  waiting for transfers between devices  65.8 us (16%)
  local copies, waits for them, and re-layouts  23 us (6%)
  between operations  17.9 us (4%)
  matrix products  15.3 us (4%)
    scatter-add x1, other arithmetic, on_device(): jax.ops.segment_sum(summed.reshape(-1), flat_labels, num_segments=LABELS)  114 us
    psum x1, blocking collectives, on_device(): total = lax.psum(binned, 'space')  75.7 us
    ppermute x11, starting transfers between devices, extended(): lax.ppermute(lax.slice_in_dim(block, block.shape[dim] - width, None, axis...  60.2 us
    all_gather x1, waiting for transfers between devices, on_device(): shards = lax.all_gather(weighted, 'exp', axis=0, tiled=False)  59.2 us
    ppermute x11, starting transfers between devices, extended(): lax.ppermute(lax.slice_in_dim(block, 0, width, axis=dim), axis, backward)  14.8 us
    scatter-add x5, local copies, waits for them, and re-layouts, on_device(): state = state.at[0].add(pulse)  11 us
    concatenate x11, other arithmetic, extended(): block = jnp.concatenate([low, block, high], axis=dim)  9.36 us
    dot_general x5, matrix products, on_device(): jnp.einsum('dc,dxyz->cxyz', mixing, adjoint, precision=lax.Precision.HIGH...  9.34 us
  transfers between devices with their start and end apart: 23, of which 3 were waited for; matrix products, arithmetic and copies ran while one was open for 13% of the time, Pallas kernels for 0%

profile of v1, /device:TPU:24, one launch (start us, length us, event | category | flops | bytes accessed | tf_op | source)
XLA Modules:
  0.0 409.4 jit_solution(14453021140694918377)
XLA Ops:
  7.2 0.8 fusion.79
  8.1 3.5 collective-permute-start.2
  11.6 1.3 collective-permute-start
  12.9 1.1 copy.46
  14.1 4.6 %collective-permute-start.13 = (f32[4,1,64,128]{3,0,2,1:T(4,128)S(1)}, f32[4,1,64,128]{3,0,2,1:T(4,128)S(1)}, u32[]{:S(2)}, u32[]{:S(2)}) collective-permute-start(f32[4,1,64,128]{3,0,2,1:T(4,128)S(1)} %get-tuple-element.81), channel_id=1, source_target_pairs={{0,1},{1,2},{2,3},{3,4},{4,5},{5,6},{6,7},{7,8},{8,9},{9,10},{10,1... | collective-permute-start | bytes 393224 | tf_op jit(solution)/shard_map/ppermute | solution.py:17
  18.6 1.3 collective-permute-start.12
  20.1 4.6 %collective-permute-start.3 = (f32[4,1,64,128]{3,0,2,1:T(4,128)S(1)}, f32[4,1,64,128]{3,0,2,1:T(4,128)S(1)}, u32[]{:S(2)}, u32[]{:S(2)}) collective-permute-start(f32[4,1,64,128]{3,0,2,1:T(4,128)S(1)} %get-tuple-element.91), channel_id=1, source_target_pairs={{0,1},{1,2},{2,3},{3,4},{4,5},{5,6},{6,7},{7,8},{8,9},{9,10},{10,1... | collective-permute-start | bytes 393224 | tf_op jit(solution)/shard_map/ppermute | solution.py:17
  26.9 1.3 collective-permute-start.1
  28.6 5.2 %collective-permute-done.1 = f32[4,1,64,128]{3,0,2,1:T(4,128)S(1)} collective-permute-done((f32[4,1,64,128]{3,0,2,1:T(4,128)S(1)}, f32[4,1,64,128]{3,0,2,1:T(4,128)S(1)}, u32[]{:S(2)}, u32[]{:S(2)}) %collective-permute-start.1) | collective-permute-done | bytes 131104 | tf_op jit(solution)/shard_map/ppermute | solution.py:20
  34.4 0.8 fusion.20
  35.4 1.3 scatter-add.24
  36.8 5.0 %collective-permute-start.5 = (f32[4,1,64,128]{3,0,2,1:T(4,128)S(1)}, f32[4,1,64,128]{3,0,2,1:T(4,128)S(1)}, u32[]{:S(2)}, u32[]{:S(2)}) collective-permute-start(f32[4,1,64,128]{3,0,2,1:T(4,128)S(1)} %get-tuple-element.89), channel_id=1, source_target_pairs={{0,1},{1,2},{2,3},{3,4},{4,5},{5,6},{6,7},{7,8},{8,9},{9,10},{10,1... | collective-permute-start | bytes 393224 | tf_op jit(solution)/shard_map/ppermute | solution.py:17
  41.7 1.3 collective-permute-start.4
  43.8 1.1 fusion.10
  45.0 0.7 fusion.72
  45.7 7.3 %collective-permute-start.15 = (f32[4,1,64,128]{3,0,2,1:T(4,128)}, f32[4,1,64,128]{3,0,2,1:T(4,128)}, u32[]{:S(2)}, u32[]{:S(2)}) collective-permute-start(f32[4,1,64,128]{3,0,2,1:T(4,128)} %get-tuple-element.79), channel_id=1, source_target_pairs={{0,1},{1,2},{2,3},{3,4},{4,5},{5,6},{6,7},{7,8},{8,9},{9,10},{10,1... | collective-permute-start | bytes 393224 | tf_op jit(solution)/shard_map/ppermute | solution.py:17
  53.0 1.3 collective-permute-start.14
  55.0 1.0 fusion.18
  56.7 0.8 slice_add_fusion.3
  57.5 2.8 scatter-add.25
  60.3 1.0 fusion.76
  61.4 6.0 %collective-permute-start.7 = (f32[4,1,64,128]{3,0,2,1:T(4,128)S(1)}, f32[4,1,64,128]{3,0,2,1:T(4,128)S(1)}, u32[]{:S(2)}, u32[]{:S(2)}) collective-permute-start(f32[4,1,64,128]{3,0,2,1:T(4,128)S(1)} %get-tuple-element.87), channel_id=1, source_target_pairs={{0,1},{1,2},{2,3},{3,4},{4,5},{5,6},{6,7},{7,8},{8,9},{9,10},{10,1... | collective-permute-start | bytes 393224 | tf_op jit(solution)/shard_map/ppermute | solution.py:17
  67.4 1.3 collective-permute-start.6
  68.8 1.7 select_maximum_fusion.6
  70.5 2.6 fusion.8
  73.1 0.8 fusion.71
  73.9 5.2 %collective-permute-start.17 = (f32[4,1,64,128]{3,0,2,1:T(4,128)}, f32[4,1,64,128]{3,0,2,1:T(4,128)}, u32[]{:S(2)}, u32[]{:S(2)}) collective-permute-start(f32[4,1,64,128]{3,0,2,1:T(4,128)} %get-tuple-element.77), channel_id=1, source_target_pairs={{0,1},{1,2},{2,3},{3,4},{4,5},{5,6},{6,7},{7,8},{8,9},{9,10},{10,1... | collective-permute-start | bytes 393224 | tf_op jit(solution)/shard_map/ppermute | solution.py:17
  79.1 1.5 collective-permute-start.16
  81.2 1.0 fusion.16
  82.9 0.8 slice_add_fusion.2
  83.7 2.8 scatter-add.26
  86.6 1.0 fusion.75
  87.6 4.6 %collective-permute-start.9 = (f32[4,1,64,128]{3,0,2,1:T(4,128)S(1)}, f32[4,1,64,128]{3,0,2,1:T(4,128)S(1)}, u32[]{:S(2)}, u32[]{:S(2)}) collective-permute-start(f32[4,1,64,128]{3,0,2,1:T(4,128)S(1)} %get-tuple-element.85), channel_id=1, source_target_pairs={{0,1},{1,2},{2,3},{3,4},{4,5},{5,6},{6,7},{7,8},{8,9},{9,10},{10,1... | collective-permute-start | bytes 393224 | tf_op jit(solution)/shard_map/ppermute | solution.py:17
  92.2 1.3 collective-permute-start.8
  93.5 1.7 select_maximum_fusion.4
  95.3 2.3 fusion.6
  97.5 0.8 fusion.70
  98.3 6.8 %collective-permute-start.19 = (f32[4,1,64,128]{3,0,2,1:T(4,128)}, f32[4,1,64,128]{3,0,2,1:T(4,128)}, u32[]{:S(2)}, u32[]{:S(2)}) collective-permute-start(f32[4,1,64,128]{3,0,2,1:T(4,128)} %get-tuple-element.75), channel_id=1, source_target_pairs={{0,1},{1,2},{2,3},{3,4},{4,5},{5,6},{6,7},{7,8},{8,9},{9,10},{10,1... | collective-permute-start | bytes 393224 | tf_op jit(solution)/shard_map/ppermute | solution.py:17
  105.1 1.4 collective-permute-start.18
  106.5 2.5 multiply_reduce_fusion.2
  109.7 1.0 fusion.14
  111.4 0.8 slice_add_fusion.1
  112.2 2.8 scatter-add.29
  115.0 1.0 fusion.74
  116.1 6.0 %collective-permute-start.11 = (f32[4,1,64,128]{3,0,2,1:T(4,128)S(1)}, f32[4,1,64,128]{3,0,2,1:T(4,128)S(1)}, u32[]{:S(2)}, u32[]{:S(2)}) collective-permute-start(f32[4,1,64,128]{3,0,2,1:T(4,128)S(1)} %get-tuple-element.83), channel_id=1, source_target_pairs={{0,1},{1,2},{2,3},{3,4},{4,5},{5,6},{6,7},{7,8},{8,9},{9,10},{10,1... | collective-permute-start | bytes 393224 | tf_op jit(solution)/shard_map/ppermute | solution.py:17
  122.1 1.3 collective-permute-start.10
  123.4 1.7 select_maximum_fusion.2
  125.2 2.3 fusion.4
  127.6 6.7 %collective-permute-start.21 = (f32[4,1,64,128]{3,0,2,1:T(4,128)S(1)}, f32[4,1,64,128]{3,0,2,1:T(4,128)S(1)}, u32[]{:S(2)}, u32[]{:S(2)}) collective-permute-start(f32[4,1,64,128]{3,0,2,1:T(4,128)S(1)} %get-tuple-element.73), channel_id=1, source_target_pairs={{0,1},{1,2},{2,3},{3,4},{4,5},{5,6},{6,7},{7,8},{8,9},{9,10},{10,1... | collective-permute-start | bytes 393224 | tf_op jit(solution)/shard_map/ppermute | solution.py:17
  134.3 1.6 collective-permute-start.20
  136.0 1.9 multiply_reduce_fusion.3
  137.9 1.9 multiply_reduce_fusion.1
  141.0 0.9 multiply_reduce_fusion.4
  141.9 1.4 collective-permute-done.20
  144.0 0.9 multiply_reduce_fusion
  145.8 2.2 fusion.12
  148.2 1.3 scatter-add.36
  149.5 0.7 copy.31
  150.3 1.1 fusion.2
  151.4 0.7 copy.32
  152.1 59.2 %all-gather.3.cloned.1.call-done = f32[32,64,128]{2,1,0:T(8,128)} async-done(((f32[2,64,128]{2,1,0:T(8,128)}), f32[32,64,128]{2,1,0:T(8,128)}) %all-gather.3.cloned.1.call-update) | async-done | bytes 1048592 | tf_op jit(solution)/shard_map/all_gather | solution.py:104
  211.3 1.3 reduce_sum.69
  212.6 113.7 %scatter_custom_fusion = f32[512]{0:T(512)S(1)} fusion(s32[16384]{0:T(1024)} %bitcast.76, f32[16384]{0:T(1024)S(1)} %bitcast.75, f32[]{:T(128)} %constant.150.clone.1), kind=kCustom, calls=%fused_computation.191 | custom fusion | flops 16384 | bytes 2560 | tf_op jit(solution)/shard_map/scatter-add | solution.py:106
  326.2 75.7 %psum.7 = f32[512]{0:T(512)S(1)} all-reduce(f32[512]{0:T(512)S(1)} %scatter_custom_fusion), channel_id=1, replica_groups=mesh['exp'=16,'space'=32] {'space'}, use_global_device_ids=true, to_apply=%region_8.9 | all-reduce | flops 512 | bytes 4096 | tf_op jit(solution)/shard_map/psum | solution.py:107
  (237 shorter events, 9.6 us)
Async XLA Ops:
  7.2 12.8 %copy-start.57 = (f32[1,4,2,64,128]{4,3,2,1,0:T(8,128)S(1)}, f32[1,4,2,64,128]{4,3,2,1,0:T(8,128)}, u32[]{:S(2)}) copy-start(f32[1,4,2,64,128]{4,3,2,1,0:T(8,128)} %param.20) | copy-start | bytes 786436
  7.2 204.1 %all-gather.3.cloned.1.call-start = ((), (), s32[]{:S(2)}) async-start(), calls=%async_computation | async-start | bytes 1114112 | tf_op jit(solution)/shard_map/all_gather | solution.py:104
  8.0 16.7 %copy-start.95 = (f32[4,4]{1,0:T(4,128)S(1)}, f32[4,4]{1,0:T(4,128)}, u32[]{:S(2)}) copy-start(f32[4,4]{1,0:T(4,128)} %param.26) | copy-start | bytes 196
  8.0 16.7 %copy-start.96 = (s32[4,4]{1,0:T(4,128)S(1)}, s32[4,4]{1,0:T(4,128)}, u32[]{:S(2)}) copy-start(s32[4,4]{1,0:T(4,128)} %param.25) | copy-start | bytes 196
  8.0 20.2 %copy-start.28 = (f32[2,64,128]{2,1,0:T(8,128)S(1)}, f32[2,64,128]{2,1,0:T(8,128)}, u32[]{:S(2)}) copy-start(f32[2,64,128]{2,1,0:T(8,128)} %param.22) | copy-start | bytes 196612
  8.1 18.8 %collective-permute-start.2 = (f32[1,64,128]{2,1,0:T(8,128)S(1)}, f32[1,64,128]{2,1,0:T(8,128)S(1)}, u32[]{:S(2)}, u32[]{:S(2)}) collective-permute-start(f32[1,64,128]{2,1,0:T(8,128)S(1)} %get-tuple-element.95), channel_id=1, source_target_pairs={{0,1},{1,2},{2,3},{3,4},{4,5},{5,6},{6,7},{7,8},{8,9},{9,10},{10,1... | collective-permute-start | bytes 98312 | tf_op jit(solution)/shard_map/ppermute | solution.py:17
  11.6 16.6 %collective-permute-start = (f32[1,64,128]{2,1,0:T(8,128)S(1)}, f32[1,64,128]{2,1,0:T(8,128)S(1)}, u32[]{:S(2)}, u32[]{:S(2)}) collective-permute-start(f32[1,64,128]{2,1,0:T(8,128)S(1)} %get-tuple-element.96), channel_id=1, source_target_pairs={{1,0},{2,1},{3,2},{4,3},{5,4},{6,5},{7,6},{8,7},{9,8},{10,9},{11,1... | collective-permute-start | bytes 98312 | tf_op jit(solution)/shard_map/ppermute | solution.py:20
  14.0 29.7 %copy-start.6 = (f32[1,4,2,64,128]{4,1,3,2,0:T(4,128)}, f32[1,4,2,64,128]{4,1,3,2,0:T(4,128)S(1)}, u32[]{:S(2)}) copy-start(f32[1,4,2,64,128]{4,1,3,2,0:T(4,128)S(1)} %copy.46) | copy-start | bytes 786436
  14.1 29.0 %collective-permute-start.13 = (f32[4,1,64,128]{3,0,2,1:T(4,128)S(1)}, f32[4,1,64,128]{3,0,2,1:T(4,128)S(1)}, u32[]{:S(2)}, u32[]{:S(2)}) collective-permute-start(f32[4,1,64,128]{3,0,2,1:T(4,128)S(1)} %get-tuple-element.81), channel_id=1, source_target_pairs={{0,1},{1,2},{2,3},{3,4},{4,5},{5,6},{6,7},{7,8},{8,9},{9,10},{10,1... | collective-permute-start | bytes 393224 | tf_op jit(solution)/shard_map/ppermute | solution.py:17
  18.6 24.5 %collective-permute-start.12 = (f32[4,1,64,128]{3,0,2,1:T(4,128)S(1)}, f32[4,1,64,128]{3,0,2,1:T(4,128)S(1)}, u32[]{:S(2)}, u32[]{:S(2)}) collective-permute-start(f32[4,1,64,128]{3,0,2,1:T(4,128)S(1)} %get-tuple-element.82), channel_id=1, source_target_pairs={{1,0},{2,1},{3,2},{4,3},{5,4},{6,5},{7,6},{8,7},{9,8},{10,9},{11,1... | collective-permute-start | bytes 393224 | tf_op jit(solution)/shard_map/ppermute | solution.py:20
  20.1 8.4 %collective-permute-start.3 = (f32[4,1,64,128]{3,0,2,1:T(4,128)S(1)}, f32[4,1,64,128]{3,0,2,1:T(4,128)S(1)}, u32[]{:S(2)}, u32[]{:S(2)}) collective-permute-start(f32[4,1,64,128]{3,0,2,1:T(4,128)S(1)} %get-tuple-element.91), channel_id=1, source_target_pairs={{0,1},{1,2},{2,3},{3,4},{4,5},{5,6},{6,7},{7,8},{8,9},{9,10},{10,1... | collective-permute-start | bytes 393224 | tf_op jit(solution)/shard_map/ppermute | solution.py:17
  26.9 6.9 %collective-permute-start.1 = (f32[4,1,64,128]{3,0,2,1:T(4,128)S(1)}, f32[4,1,64,128]{3,0,2,1:T(4,128)S(1)}, u32[]{:S(2)}, u32[]{:S(2)}) collective-permute-start(f32[4,1,64,128]{3,0,2,1:T(4,128)S(1)} %get-tuple-element.92), channel_id=1, source_target_pairs={{1,0},{2,1},{3,2},{4,3},{5,4},{6,5},{7,6},{8,7},{9,8},{10,9},{11,1... | collective-permute-start | bytes 393224 | tf_op jit(solution)/shard_map/ppermute | solution.py:20
  28.5 15.2 %copy-start.58 = (f32[2,64,128]{2,1,0:T(8,128)}, f32[2,64,128]{2,1,0:T(8,128)S(1)}, u32[]{:S(2)}) copy-start(f32[2,64,128]{2,1,0:T(8,128)S(1)} %get-tuple-element.69) | copy-start | bytes 196612
  28.5 15.2 %copy-start.64 = (f32[2,64,128]{2,1,0:T(8,128)}, f32[2,64,128]{2,1,0:T(8,128)S(1)}, u32[]{:S(2)}) copy-start(f32[2,64,128]{2,1,0:T(8,128)S(1)} %get-tuple-element.70) | copy-start | bytes 196612
  28.5 15.2 %copy-start.70 = (f32[2,64,128]{2,1,0:T(8,128)}, f32[2,64,128]{2,1,0:T(8,128)S(1)}, u32[]{:S(2)}) copy-start(f32[2,64,128]{2,1,0:T(8,128)S(1)} %get-tuple-element.71) | copy-start | bytes 196612
  28.5 15.2 %copy-start.76 = (f32[2,64,128]{2,1,0:T(8,128)}, f32[2,64,128]{2,1,0:T(8,128)S(1)}, u32[]{:S(2)}) copy-start(f32[2,64,128]{2,1,0:T(8,128)S(1)} %get-tuple-element.72) | copy-start | bytes 196612
  28.6 15.2 %copy-start.82 = (f32[2,64,128]{2,1,0:T(8,128)}, f32[2,64,128]{2,1,0:T(8,128)S(1)}, u32[]{:S(2)}) copy-start(f32[2,64,128]{2,1,0:T(8,128)S(1)} %get-tuple-element.93) | copy-start | bytes 196612
  28.6 15.2 %copy-start.88 = (f32[2,64,128]{2,1,0:T(8,128)}, f32[2,64,128]{2,1,0:T(8,128)S(1)}, u32[]{:S(2)}) copy-start(f32[2,64,128]{2,1,0:T(8,128)S(1)} %get-tuple-element.94) | copy-start | bytes 196612
  36.8 17.5 %collective-permute-start.5 = (f32[4,1,64,128]{3,0,2,1:T(4,128)S(1)}, f32[4,1,64,128]{3,0,2,1:T(4,128)S(1)}, u32[]{:S(2)}, u32[]{:S(2)}) collective-permute-start(f32[4,1,64,128]{3,0,2,1:T(4,128)S(1)} %get-tuple-element.89), channel_id=1, source_target_pairs={{0,1},{1,2},{2,3},{3,4},{4,5},{5,6},{6,7},{7,8},{8,9},{9,10},{10,1... | collective-permute-start | bytes 393224 | tf_op jit(solution)/shard_map/ppermute | solution.py:17
  41.7 12.6 %collective-permute-start.4 = (f32[4,1,64,128]{3,0,2,1:T(4,128)S(1)}, f32[4,1,64,128]{3,0,2,1:T(4,128)S(1)}, u32[]{:S(2)}, u32[]{:S(2)}) collective-permute-start(f32[4,1,64,128]{3,0,2,1:T(4,128)S(1)} %get-tuple-element.90), channel_id=1, source_target_pairs={{1,0},{2,1},{3,2},{4,3},{5,4},{6,5},{7,6},{8,7},{9,8},{10,9},{11,1... | collective-permute-start | bytes 393224 | tf_op jit(solution)/shard_map/ppermute | solution.py:20
  43.8 10.6 %copy-start.9 = (f32[4,2,64,128]{3,0,2,1:T(4,128)S(1)}, f32[4,2,64,128]{3,0,2,1:T(4,128)}, u32[]{:S(2)}) copy-start(f32[4,2,64,128]{3,0,2,1:T(4,128)} %copy-done.8) | copy-start | bytes 786436
  44.9 10.0 %copy-start.59 = (f32[2,64,128]{2,1,0:T(8,128)S(1)}, f32[2,64,128]{2,1,0:T(8,128)}, u32[]{:S(2)}) copy-start(f32[2,64,128]{2,1,0:T(8,128)} %copy-done.58) | copy-start | bytes 196612
  44.9 10.0 %copy-start.65 = (f32[2,64,128]{2,1,0:T(8,128)S(1)}, f32[2,64,128]{2,1,0:T(8,128)}, u32[]{:S(2)}) copy-start(f32[2,64,128]{2,1,0:T(8,128)} %copy-done.64) | copy-start | bytes 196612
  45.0 10.0 %copy-start.71 = (f32[2,64,128]{2,1,0:T(8,128)S(1)}, f32[2,64,128]{2,1,0:T(8,128)}, u32[]{:S(2)}) copy-start(f32[2,64,128]{2,1,0:T(8,128)} %copy-done.70) | copy-start | bytes 196612
  45.7 23.0 %collective-permute-start.15 = (f32[4,1,64,128]{3,0,2,1:T(4,128)}, f32[4,1,64,128]{3,0,2,1:T(4,128)}, u32[]{:S(2)}, u32[]{:S(2)}) collective-permute-start(f32[4,1,64,128]{3,0,2,1:T(4,128)} %get-tuple-element.79), channel_id=1, source_target_pairs={{0,1},{1,2},{2,3},{3,4},{4,5},{5,6},{6,7},{7,8},{8,9},{9,10},{10,1... | collective-permute-start | bytes 393224 | tf_op jit(solution)/shard_map/ppermute | solution.py:17
  53.0 15.7 %collective-permute-start.14 = (f32[4,1,64,128]{3,0,2,1:T(4,128)}, f32[4,1,64,128]{3,0,2,1:T(4,128)}, u32[]{:S(2)}, u32[]{:S(2)}) collective-permute-start(f32[4,1,64,128]{3,0,2,1:T(4,128)} %get-tuple-element.80), channel_id=1, source_target_pairs={{1,0},{2,1},{3,2},{4,3},{5,4},{6,5},{7,6},{8,7},{9,8},{10,9},{11,1... | collective-permute-start | bytes 393224 | tf_op jit(solution)/shard_map/ppermute | solution.py:20
  60.3 10.1 %copy-start.20 = (f32[4,2,64,128]{3,0,2,1:T(4,128)S(1)}, f32[4,2,64,128]{3,0,2,1:T(4,128)}, u32[]{:S(2)}) copy-start(f32[4,2,64,128]{3,0,2,1:T(4,128)} %copy-done.19) | copy-start | bytes 786436
  60.3 10.1 %copy-start.60 = (f32[2,64,128]{2,1,0:T(8,128)S(1)}, f32[2,64,128]{2,1,0:T(8,128)}, u32[]{:S(2)}) copy-start(f32[2,64,128]{2,1,0:T(8,128)} %copy-done.58) | copy-start | bytes 196612
  60.3 10.1 %copy-start.66 = (f32[2,64,128]{2,1,0:T(8,128)S(1)}, f32[2,64,128]{2,1,0:T(8,128)}, u32[]{:S(2)}) copy-start(f32[2,64,128]{2,1,0:T(8,128)} %copy-done.64) | copy-start | bytes 196612
  60.3 10.1 %copy-start.72 = (f32[2,64,128]{2,1,0:T(8,128)S(1)}, f32[2,64,128]{2,1,0:T(8,128)}, u32[]{:S(2)}) copy-start(f32[2,64,128]{2,1,0:T(8,128)} %copy-done.70) | copy-start | bytes 196612
  60.3 10.1 %copy-start.78 = (f32[2,64,128]{2,1,0:T(8,128)S(1)}, f32[2,64,128]{2,1,0:T(8,128)}, u32[]{:S(2)}) copy-start(f32[2,64,128]{2,1,0:T(8,128)} %copy-done.76) | copy-start | bytes 196612
  60.3 10.1 %copy-start.84 = (f32[2,64,128]{2,1,0:T(8,128)S(1)}, f32[2,64,128]{2,1,0:T(8,128)}, u32[]{:S(2)}) copy-start(f32[2,64,128]{2,1,0:T(8,128)} %copy-done.82) | copy-start | bytes 196612
  60.3 10.1 %copy-start.90 = (f32[2,64,128]{2,1,0:T(8,128)S(1)}, f32[2,64,128]{2,1,0:T(8,128)}, u32[]{:S(2)}) copy-start(f32[2,64,128]{2,1,0:T(8,128)} %copy-done.88) | copy-start | bytes 196612
  61.4 19.1 %collective-permute-start.7 = (f32[4,1,64,128]{3,0,2,1:T(4,128)S(1)}, f32[4,1,64,128]{3,0,2,1:T(4,128)S(1)}, u32[]{:S(2)}, u32[]{:S(2)}) collective-permute-start(f32[4,1,64,128]{3,0,2,1:T(4,128)S(1)} %get-tuple-element.87), channel_id=1, source_target_pairs={{0,1},{1,2},{2,3},{3,4},{4,5},{5,6},{6,7},{7,8},{8,9},{9,10},{10,1... | collective-permute-start | bytes 393224 | tf_op jit(solution)/shard_map/ppermute | solution.py:17
  67.4 13.1 %collective-permute-start.6 = (f32[4,1,64,128]{3,0,2,1:T(4,128)S(1)}, f32[4,1,64,128]{3,0,2,1:T(4,128)S(1)}, u32[]{:S(2)}, u32[]{:S(2)}) collective-permute-start(f32[4,1,64,128]{3,0,2,1:T(4,128)S(1)} %get-tuple-element.88), channel_id=1, source_target_pairs={{1,0},{2,1},{3,2},{4,3},{5,4},{6,5},{7,6},{8,7},{9,8},{10,9},{11,1... | collective-permute-start | bytes 393224 | tf_op jit(solution)/shard_map/ppermute | solution.py:20
  70.5 10.1 %copy-start.12 = (f32[4,2,64,128]{3,0,2,1:T(4,128)S(1)}, f32[4,2,64,128]{3,0,2,1:T(4,128)}, u32[]{:S(2)}) copy-start(f32[4,2,64,128]{3,0,2,1:T(4,128)} %scatter-add.25) | copy-start | bytes 786436
  73.9 19.6 %collective-permute-start.17 = (f32[4,1,64,128]{3,0,2,1:T(4,128)}, f32[4,1,64,128]{3,0,2,1:T(4,128)}, u32[]{:S(2)}, u32[]{:S(2)}) collective-permute-start(f32[4,1,64,128]{3,0,2,1:T(4,128)} %get-tuple-element.77), channel_id=1, source_target_pairs={{0,1},{1,2},{2,3},{3,4},{4,5},{5,6},{6,7},{7,8},{8,9},{9,10},{10,1... | collective-permute-start | bytes 393224 | tf_op jit(solution)/shard_map/ppermute | solution.py:17
  79.1 14.4 %collective-permute-start.16 = (f32[4,1,64,128]{3,0,2,1:T(4,128)}, f32[4,1,64,128]{3,0,2,1:T(4,128)}, u32[]{:S(2)}, u32[]{:S(2)}) collective-permute-start(f32[4,1,64,128]{3,0,2,1:T(4,128)} %get-tuple-element.78), channel_id=1, source_target_pairs={{1,0},{2,1},{3,2},{4,3},{5,4},{6,5},{7,6},{8,7},{9,8},{10,9},{11,1... | collective-permute-start | bytes 393224 | tf_op jit(solution)/shard_map/ppermute | solution.py:20
  87.6 21.4 %collective-permute-start.9 = (f32[4,1,64,128]{3,0,2,1:T(4,128)S(1)}, f32[4,1,64,128]{3,0,2,1:T(4,128)S(1)}, u32[]{:S(2)}, u32[]{:S(2)}) collective-permute-start(f32[4,1,64,128]{3,0,2,1:T(4,128)S(1)} %get-tuple-element.85), channel_id=1, source_target_pairs={{0,1},{1,2},{2,3},{3,4},{4,5},{5,6},{6,7},{7,8},{8,9},{9,10},{10,1... | collective-permute-start | bytes 393224 | tf_op jit(solution)/shard_map/ppermute | solution.py:17
  92.2 16.9 %collective-permute-start.8 = (f32[4,1,64,128]{3,0,2,1:T(4,128)S(1)}, f32[4,1,64,128]{3,0,2,1:T(4,128)S(1)}, u32[]{:S(2)}, u32[]{:S(2)}) collective-permute-start(f32[4,1,64,128]{3,0,2,1:T(4,128)S(1)} %get-tuple-element.86), channel_id=1, source_target_pairs={{1,0},{2,1},{3,2},{4,3},{5,4},{6,5},{7,6},{8,7},{9,8},{10,9},{11,1... | collective-permute-start | bytes 393224 | tf_op jit(solution)/shard_map/ppermute | solution.py:20
  95.2 11.3 %copy-start.5 = (f32[4,4,66,130]{3,0,2,1:T(4,128)S(1)}, f32[4,4,66,130]{3,0,2,1:T(4,128)}, u32[]{:S(2)}) copy-start(f32[4,4,66,130]{3,0,2,1:T(4,128)} %copy-done.4) | copy-start | bytes 1647364
  95.2 11.3 %copy-start.13 = (f32[4,2,64,128]{3,0,2,1:T(4,128)S(1)}, f32[4,2,64,128]{3,0,2,1:T(4,128)}, u32[]{:S(2)}) copy-start(f32[4,2,64,128]{3,0,2,1:T(4,128)} %scatter-add.25) | copy-start | bytes 786436
  95.2 11.3 %copy-start.53 = (f32[4,1,64,128]{3,0,2,1:T(4,128)S(1)}, f32[4,1,64,128]{3,0,2,1:T(4,128)}, u32[]{:S(2)}) copy-start(f32[4,1,64,128]{3,0,2,1:T(4,128)} %copy-done.52) | copy-start | bytes 393220
  95.2 11.3 %copy-start.55 = (f32[4,1,64,128]{3,0,2,1:T(4,128)S(1)}, f32[4,1,64,128]{3,0,2,1:T(4,128)}, u32[]{:S(2)}) copy-start(f32[4,1,64,128]{3,0,2,1:T(4,128)} %copy-done.54) | copy-start | bytes 393220
  98.3 25.1 %collective-permute-start.19 = (f32[4,1,64,128]{3,0,2,1:T(4,128)}, f32[4,1,64,128]{3,0,2,1:T(4,128)}, u32[]{:S(2)}, u32[]{:S(2)}) collective-permute-start(f32[4,1,64,128]{3,0,2,1:T(4,128)} %get-tuple-element.75), channel_id=1, source_target_pairs={{0,1},{1,2},{2,3},{3,4},{4,5},{5,6},{6,7},{7,8},{8,9},{9,10},{10,1... | collective-permute-start | bytes 393224 | tf_op jit(solution)/shard_map/ppermute | solution.py:17
  105.1 18.4 %collective-permute-start.18 = (f32[4,1,64,128]{3,0,2,1:T(4,128)}, f32[4,1,64,128]{3,0,2,1:T(4,128)}, u32[]{:S(2)}, u32[]{:S(2)}) collective-permute-start(f32[4,1,64,128]{3,0,2,1:T(4,128)} %get-tuple-element.76), channel_id=1, source_target_pairs={{1,0},{2,1},{3,2},{4,3},{5,4},{6,5},{7,6},{8,7},{9,8},{10,9},{11,1... | collective-permute-start | bytes 393224 | tf_op jit(solution)/shard_map/ppermute | solution.py:20
  115.0 10.1 %copy-start.25 = (f32[4,2,64,128]{3,0,2,1:T(4,128)S(1)}, f32[4,2,64,128]{3,0,2,1:T(4,128)}, u32[]{:S(2)}) copy-start(f32[4,2,64,128]{3,0,2,1:T(4,128)} %copy-done.24) | copy-start | bytes 786436
  115.0 10.1 %copy-start.62 = (f32[2,64,128]{2,1,0:T(8,128)S(1)}, f32[2,64,128]{2,1,0:T(8,128)}, u32[]{:S(2)}) copy-start(f32[2,64,128]{2,1,0:T(8,128)} %copy-done.58) | copy-start | bytes 196612
  115.0 10.1 %copy-start.68 = (f32[2,64,128]{2,1,0:T(8,128)S(1)}, f32[2,64,128]{2,1,0:T(8,128)}, u32[]{:S(2)}) copy-start(f32[2,64,128]{2,1,0:T(8,128)} %copy-done.64) | copy-start | bytes 196612
  115.0 10.2 %copy-start.74 = (f32[2,64,128]{2,1,0:T(8,128)S(1)}, f32[2,64,128]{2,1,0:T(8,128)}, u32[]{:S(2)}) copy-start(f32[2,64,128]{2,1,0:T(8,128)} %copy-done.70) | copy-start | bytes 196612
  115.0 10.2 %copy-start.80 = (f32[2,64,128]{2,1,0:T(8,128)S(1)}, f32[2,64,128]{2,1,0:T(8,128)}, u32[]{:S(2)}) copy-start(f32[2,64,128]{2,1,0:T(8,128)} %copy-done.76) | copy-start | bytes 196612
  115.0 10.2 %copy-start.86 = (f32[2,64,128]{2,1,0:T(8,128)S(1)}, f32[2,64,128]{2,1,0:T(8,128)}, u32[]{:S(2)}) copy-start(f32[2,64,128]{2,1,0:T(8,128)} %copy-done.82) | copy-start | bytes 196612
  115.0 10.2 %copy-start.92 = (f32[2,64,128]{2,1,0:T(8,128)S(1)}, f32[2,64,128]{2,1,0:T(8,128)}, u32[]{:S(2)}) copy-start(f32[2,64,128]{2,1,0:T(8,128)} %copy-done.88) | copy-start | bytes 196612
  116.1 23.8 %collective-permute-start.11 = (f32[4,1,64,128]{3,0,2,1:T(4,128)S(1)}, f32[4,1,64,128]{3,0,2,1:T(4,128)S(1)}, u32[]{:S(2)}, u32[]{:S(2)}) collective-permute-start(f32[4,1,64,128]{3,0,2,1:T(4,128)S(1)} %get-tuple-element.83), channel_id=1, source_target_pairs={{0,1},{1,2},{2,3},{3,4},{4,5},{5,6},{6,7},{7,8},{8,9},{9,10},{10,1... | collective-permute-start | bytes 393224 | tf_op jit(solution)/shard_map/ppermute | solution.py:17
  122.1 17.7 %collective-permute-start.10 = (f32[4,1,64,128]{3,0,2,1:T(4,128)S(1)}, f32[4,1,64,128]{3,0,2,1:T(4,128)S(1)}, u32[]{:S(2)}, u32[]{:S(2)}) collective-permute-start(f32[4,1,64,128]{3,0,2,1:T(4,128)S(1)} %get-tuple-element.84), channel_id=1, source_target_pairs={{1,0},{2,1},{3,2},{4,3},{5,4},{6,5},{7,6},{8,7},{9,8},{10,9},{11,1... | collective-permute-start | bytes 393224 | tf_op jit(solution)/shard_map/ppermute | solution.py:20
  125.2 10.8 %copy-start.1 = (f32[4,4,66,130]{3,0,2,1:T(4,128)S(1)}, f32[4,4,66,130]{3,0,2,1:T(4,128)}, u32[]{:S(2)}) copy-start(f32[4,4,66,130]{3,0,2,1:T(4,128)} %copy-done) | copy-start | bytes 1647364
  125.2 10.8 %copy-start.3 = (f32[4,4,66,130]{3,0,2,1:T(4,128)S(1)}, f32[4,4,66,130]{3,0,2,1:T(4,128)}, u32[]{:S(2)}) copy-start(f32[4,4,66,130]{3,0,2,1:T(4,128)} %copy-done.2) | copy-start | bytes 1647364
  125.2 10.8 %copy-start.16 = (f32[4,2,64,128]{3,0,2,1:T(4,128)S(1)}, f32[4,2,64,128]{3,0,2,1:T(4,128)}, u32[]{:S(2)}) copy-start(f32[4,2,64,128]{3,0,2,1:T(4,128)} %scatter-add.26) | copy-start | bytes 786436
  125.2 10.8 %copy-start.21 = (f32[4,2,64,128]{3,0,2,1:T(4,128)S(1)}, f32[4,2,64,128]{3,0,2,1:T(4,128)}, u32[]{:S(2)}) copy-start(f32[4,2,64,128]{3,0,2,1:T(4,128)} %copy-done.19) | copy-start | bytes 786436
  125.2 10.8 %copy-start.49 = (f32[4,1,64,128]{3,0,2,1:T(4,128)S(1)}, f32[4,1,64,128]{3,0,2,1:T(4,128)}, u32[]{:S(2)}) copy-start(f32[4,1,64,128]{3,0,2,1:T(4,128)} %copy-done.48) | copy-start | bytes 393220
  125.2 10.8 %copy-start.51 = (f32[4,1,64,128]{3,0,2,1:T(4,128)S(1)}, f32[4,1,64,128]{3,0,2,1:T(4,128)}, u32[]{:S(2)}) copy-start(f32[4,1,64,128]{3,0,2,1:T(4,128)} %copy-done.50) | copy-start | bytes 393220
  127.5 16.5 %copy-start.22 = (f32[4,2,64,128]{3,0,2,1:T(4,128)}, f32[4,2,64,128]{3,0,2,1:T(4,128)S(1)}, u32[]{:S(2)}) copy-start(f32[4,2,64,128]{3,0,2,1:T(4,128)S(1)} %fusion.4) | copy-start | bytes 786436
  127.6 14.3 %collective-permute-start.21 = (f32[4,1,64,128]{3,0,2,1:T(4,128)S(1)}, f32[4,1,64,128]{3,0,2,1:T(4,128)S(1)}, u32[]{:S(2)}, u32[]{:S(2)}) collective-permute-start(f32[4,1,64,128]{3,0,2,1:T(4,128)S(1)} %get-tuple-element.73), channel_id=1, source_target_pairs={{0,1},{1,2},{2,3},{3,4},{4,5},{5,6},{6,7},{7,8},{8,9},{9,10},{10,1... | collective-permute-start | bytes 393224 | tf_op jit(solution)/shard_map/ppermute | solution.py:17
  134.3 9.1 %collective-permute-start.20 = (f32[4,1,64,128]{3,0,2,1:T(4,128)S(1)}, f32[4,1,64,128]{3,0,2,1:T(4,128)S(1)}, u32[]{:S(2)}, u32[]{:S(2)}) collective-permute-start(f32[4,1,64,128]{3,0,2,1:T(4,128)S(1)} %get-tuple-element.74), channel_id=1, source_target_pairs={{1,0},{2,1},{3,2},{4,3},{5,4},{6,5},{7,6},{8,7},{9,8},{10,9},{11,1... | collective-permute-start | bytes 393224 | tf_op jit(solution)/shard_map/ppermute | solution.py:20
  (56 other events, 233.0 us)
Sparse Core Ops, SparseCore 0:
  145.8 65.4 all-gather.2
